TPU v7x, 32 devices: a whole 2x2x4 slice. The times are simulated.
32 devices in a mesh: boot: 2 (over x), samp: 16 (over z, y, core).
Axes of the slice: x: 2, y: 2, z: 4, core: 2. Of those that a mesh axis runs over, the one named last changes fastest.
Arguments:
- dosage: bfloat16 [32384, 512], P('samp'), may hold values from 0 to 2, as said below
- residuals: bfloat16 [32384, 1280], P('samp', 'boot'), may hold values from -300 to 300
- maf_bin: int32 [512], replicated, may hold values from 0 to 63
- gene_map: int32 [512], replicated, may hold values from 0 to 31, never falling along the last dimension, each value on 1 to 32 neighbouring positions
- gene_order: int32 [32], replicated, may hold values from 0 to 31, each once
Outputs:
- calibrated: float32 [32, 1280], P('samp', 'boot')
Inputs may be any that keep to these rules, and one draw needn't show every extreme that they name: `dosage`: allele counts 0, 1 or 2. `gene_map`: never falling along the variants; each gene holds 1 to 32 consecutive variants, one gene exactly 32. `gene_order`: each gene once.
All inputs are finite; a program needn't handle non-finite values.
Results may differ from a plain program's by a relative error of at most 0.0003.
Values sent between devices are 32-bit elements; how exact they have to be, the bound alone decides.
A program may use at most 64 MiB of HBM per device.

v0:
```python
import math

import jax
import jax.numpy as jnp
from jax import lax
from jax.sharding import PartitionSpec as P

GENE_DEV = 2
RHOS = 11
MAF_BINS = 64


EPSILON = 1e-05


def variant_weights(maf_bin):
    levels = jnp.arange(MAF_BINS, dtype=jnp.float32)
    weight_table = (1.0 - 0.05 * (levels + 0.5) / MAF_BINS) ** 24
    matches = maf_bin[:, None] == jnp.arange(MAF_BINS, dtype=jnp.int32)[None, :]
    return jnp.sum(
        jnp.where(matches, weight_table[None, :], jnp.zeros_like(weight_table)[None, :]), axis=1
    )


def sample_product(dose_part, residuals):
    return lax.dot_general(
        dose_part, residuals, (((0,), (0,)), ((), ())), preferred_element_type=jnp.float32
    )


def shards(dosage, residuals, maf_bin, gene_map, gene_order):
    sample_total = dosage.shape[0] * lax.axis_size("samp")
    scaling = variant_weights(maf_bin) / math.sqrt(sample_total)
    my_index = lax.axis_index("samp")
    partial_value = sample_product(dosage, residuals) * scaling[:, None]
    scores = lax.psum(partial_value, "samp")
    owned_genes = lax.dynamic_slice_in_dim(gene_order, my_index * GENE_DEV, GENE_DEV)
    member = (owned_genes[:, None] == gene_map[None, :]).astype(jnp.float32)
    stacked = jnp.concatenate([scores, scores * scores], axis=1)
    gene_sums = jnp.dot(
        member, stacked, precision=lax.Precision.HIGHEST, preferred_element_type=jnp.float32
    )
    boot_local = residuals.shape[1]
    burden = gene_sums[:, :boot_local]
    skat = gene_sums[:, boot_local:]
    rho_grid = jnp.arange(RHOS, dtype=jnp.float32) / (RHOS - 1)
    mixtures = (1.0 - rho_grid)[None, :, None] * skat[:, None, :] + rho_grid[None, :, None] * (
        burden * burden
    )[:, None, :]
    boot_total = boot_local * lax.axis_size("boot")
    first_sum, square_sum = lax.psum(
        (jnp.sum(mixtures, axis=2), jnp.sum(mixtures * mixtures, axis=2)), "boot"
    )
    center = first_sum / boot_total
    spread = square_sum / boot_total - center * center
    deviation = mixtures - center[:, :, None]
    zscore = deviation / jnp.sqrt(spread[:, :, None] + EPSILON)
    return jnp.max(zscore, axis=1)


def solution(mesh):
    placed = (P("samp", None), P("samp", "boot"), P(), P(), P())
    return jax.shard_map(
        shards, mesh=mesh, in_specs=placed, out_specs=P("samp", "boot"), check_vma=False
    )
```

profile of v0, /device:TPU:0, one launch (start us, length us, event | category | flops | bytes accessed | tf_op | source)
XLA Modules:
  0.0 128.8 jit_solution(401770869329293279)
XLA Ops:
  6.5 0.0 copy-start
  6.5 0.0 all-reduce.3.cloned.1.call-start
  6.6 0.9 select_reduce_fusion
  7.5 0.8 copy-done
  8.3 0.0 copy-start.3
  8.3 4.5 %convolution_multiply_fusion = f32[512,640]{1,0:T(8,128)} fusion(bf16[2024,512]{1,0:T(8,128)(2,1)} %param.5, bf16[2024,640]{1,0:T(8,128)(2,1)S(1)} %copy-done, f32[512]{0:T(512)S(1)} %broadcast_multiply_fusion.1), kind=kOutput, calls=%fused_computation.4 | convolution fusion | flops 1326776320 | bytes 5976064 | tf_op jit(solution)/shard_map/dot_general | solution.py:26
  12.8 0.0 all-reduce.3.cloned.1.call-update
  12.8 0.0 copy-start.2
  12.8 0.0 copy-done.3
  12.9 0.1 dynamic_slice.3
  12.9 96.9 %all-reduce.3.cloned.1.call-done = f32[512,640]{1,0:T(8,128)} async-done(((f32[512,640]{1,0:T(8,128)}), f32[512,640]{1,0:T(8,128)}) %all-reduce.3.cloned.1.call-update) | async-done | bytes 1310736 | tf_op jit(solution)/shard_map/psum | solution.py:36
  109.8 0.0 copy-start.1
  109.8 1.9 %mul.96 = f32[512,640]{1,0:T(8,128)S(1)} multiply(f32[512,640]{1,0:T(8,128)} %all-reduce.3.cloned.1.call-done, f32[512,640]{1,0:T(8,128)} %all-reduce.3.cloned.1.call-done) | non-fusion elementwise | flops 327680 | bytes 3932160 | tf_op jit(solution)/shard_map/mul | solution.py:39
  111.7 0.0 copy-done.2
  111.8 0.1 copy-done.1
  111.9 1.0 fusion
  112.9 0.2 fusion.5
  113.1 8.1 %all-reduce = (f32[2,11]{0,1:T(8,128)S(1)}, f32[2,11]{0,1:T(8,128)S(1)}) all-reduce(f32[2,11]{0,1:T(8,128)S(1)} %get-tuple-element.6, f32[2,11]{0,1:T(8,128)S(1)} %get-tuple-element.5), channel_id=1, replica_groups=mesh['boot'=2,'samp'=16] {'boot'}, use_global_device_ids=true, to_apply=%region_5.6 | all-reduce | flops 44 | bytes 352 | tf_op jit(solution)/shard_map/psum | solution.py:51
  121.2 0.7 fusion.4
  (5 shorter events, 0.0 us)
Async XLA Ops:
  6.5 1.7 %copy-start = (bf16[2024,640]{1,0:T(8,128)(2,1)S(1)}, bf16[2024,640]{1,0:T(8,128)(2,1)}, u32[]{:S(2)}) copy-start(bf16[2024,640]{1,0:T(8,128)(2,1)} %param.6) | copy-start | bytes 7772164
  6.5 103.3 %all-reduce.3.cloned.1.call-start = ((), (), s32[]{:S(2)}) async-start(), calls=%async_computation | async-start | bytes 2621440 | tf_op jit(solution)/shard_map/psum | solution.py:36
  8.3 4.6 %copy-start.3 = (s32[32]{0:T(128)S(1)}, s32[32]{0:T(128)}, u32[]{:S(2)}) copy-start(s32[32]{0:T(128)} %param.9) | copy-start | bytes 388
  12.8 98.9 %copy-start.2 = (s32[512]{0:T(512)S(1)}, s32[512]{0:T(512)}, u32[]{:S(2)}) copy-start(s32[512]{0:T(512)} %param.8) | copy-start | bytes 6148
  109.8 2.1 %copy-start.1 = (f32[512,640]{1,0:T(8,128)S(1)}, f32[512,640]{1,0:T(8,128)}, u32[]{:S(2)}) copy-start(f32[512,640]{1,0:T(8,128)} %all-reduce.3.cloned.1.call-done) | copy-start | bytes 3932164
Sparse Core Ops, SparseCore 0:
  12.9 96.7 all-reduce.2
where the time goes:
time: 129 us
  waiting for transfers between devices  96.9 us (75%)
  between operations  13.4 us (10%)
  blocking collectives  8.14 us (6%)
  matrix products  5.49 us (4%)
  other arithmetic  3.86 us (3%)
    psum x1, waiting for transfers between devices, shards(): scores = lax.psum(partial_value, 'samp')  96.9 us
    psum x1, blocking collectives, shards(): lax.psum((jnp.sum(mixtures, axis=2), jnp.sum(mixtures * mixtures, axis=2)...  8.14 us
    dot_general x1, matrix products, sample_product(): lax.dot_general(dose_part, residuals, (((0,), (0,)), ((), ())), preferred...  4.52 us
  transfers between devices with their start and end apart: 1, of which 1 were waited for; matrix products, arithmetic and copies ran while one was open for 0% of the time, Pallas kernels for 0%

commit v1 on v0

v1 whole, which is shorter than its diff:
```python
import functools

import jax
import jax.numpy as jnp
from jax import lax
from jax.experimental import pallas as pl
from jax.experimental.pallas import tpu as pltpu
from jax.sharding import PartitionSpec as P

RHOS = 11
MAF_BINS = 64
EPSILON = 1e-05
CHUNKS = 4
MESH = pl.DeviceIdType.MESH


def up(value, unit):
    return (value + unit - 1) // unit * unit


def kernel(
    n_boot,
    n_samp,
    rows,
    half,
    dose_hbm,
    resid_hbm,
    maf_ref,
    map_ref,
    order_ref,
    out_ref,
    dose,
    resid,
    acc,
    *rest,
):
    levels = n_samp.bit_length() - 1
    landed = rest[:levels]
    stacked, block, gathered = rest[levels:levels + 3]
    load_sem, send_sem, recv_sem, spread_send, spread_recv = rest[levels + 3:]
    devices = n_boot * n_samp
    variants = dose.shape[1]
    width = variants // CHUNKS
    genes = order_ref.shape[1]
    gene_dev = genes // n_samp
    rows_p = acc.shape[2]
    my_boot = lax.axis_index("boot")
    me = lax.axis_index("samp")
    linear = my_boot * n_samp + me

    loads = [pltpu.make_async_copy(resid_hbm, resid, load_sem.at[0])]
    for c in range(CHUNKS):
        cols = pl.ds(c * width, width)
        loads.append(
            pltpu.make_async_copy(dose_hbm.at[:, cols], dose.at[:, cols], load_sem.at[1 + c])
        )
    for load in loads:
        load.start()

    barrier = pltpu.get_barrier_semaphore()

    def others(step):
        if devices <= 32:
            for o in range(1, devices):
                step(o)
        else:
            lax.fori_loop(1, devices, lambda o, carry: (step(o), carry)[1], 0)

    def target(o):
        other = lax.rem(linear + o, devices)
        return (other // n_samp, lax.rem(other, n_samp))

    def greet(o):
        pl.semaphore_signal(barrier, inc=1, device_id=target(o), device_id_type=MESH)

    others(greet)

    person_total = resid.shape[0] * n_samp
    base = 1.0 - 0.05 * (maf_ref[...].astype(jnp.float32) + 0.5) / MAF_BINS
    p2 = base * base
    p4 = p2 * p2
    p8 = p4 * p4
    weight = p8 * p8 * p8 / jnp.sqrt(jnp.full(base.shape, person_total, jnp.float32))
    order_row = order_ref[...].astype(jnp.float32)
    diagonal = lax.broadcasted_iota(jnp.int32, (genes, genes), 0) == lax.broadcasted_iota(
        jnp.int32, (genes, genes), 1
    )
    order_col = jnp.sum(
        jnp.where(diagonal, jnp.broadcast_to(order_row, (genes, genes)), 0.0), axis=1, keepdims=True
    )
    member = jnp.where(order_col == map_ref[...].astype(jnp.float32), 1.0, 0.0)

    bits = [lax.rem(me // (1 << t), 2) for t in range(levels)]
    lows, low = [], 0
    for t in range(levels):
        lows.append(low)
        low = low + bits[t] * (n_samp >> (t + 1))
    place = low

    def exchange(t, c):
        size = n_samp >> (t + 1)
        return pltpu.make_async_remote_copy(
            src_ref=acc.at[c, pl.ds(lows[t] + (1 - bits[t]) * size, size)],
            dst_ref=landed[t].at[c],
            send_sem=send_sem.at[t, c],
            recv_sem=recv_sem.at[t, c],
            device_id=(my_boot, me + (1 - 2 * bits[t]) * (1 << t)),
            device_id_type=MESH,
        )

    def product(c):
        loads[1 + c].wait()
        part = lax.dot_general(
            resid[...],
            dose[:, c * width:(c + 1) * width],
            (((0,), (0,)), ((), ())),
            preferred_element_type=jnp.float32,
        )
        if rows_p == rows:
            acc[c] = part.reshape(n_samp, rows, width)
        else:
            acc[c] = jnp.zeros((n_samp, rows_p, width), jnp.float32)
            for d in range(n_samp):
                acc[c, d, :rows] = part[d * rows:(d + 1) * rows]

    def fold(t, c):
        exchange(t, c).wait_recv()
        size = n_samp >> (t + 1)
        keep = pl.ds(lows[t] + bits[t] * size, size)
        acc[c, keep] = acc[c, keep] + landed[t][c]

    totals = []

    def genewise(c):
        span = slice(c * width, (c + 1) * width)
        scores = acc[c, pl.ds(place, 1)].reshape(rows_p, width) * weight[:, span]
        stacked[:rows_p] = scores * scores
        stacked[half:half + rows_p] = scores
        totals.append(
            lax.dot_general(
                member[:, span],
                stacked[...],
                (((1,), (1,)), ((), ())),
                precision=lax.Precision.HIGHEST,
                preferred_element_type=jnp.float32,
            )
        )

    stacked[...] = jnp.zeros(stacked.shape, jnp.float32)
    loads[0].wait()

    def after(t, c):
        fold(t, c)
        if t + 1 < levels:
            exchange(t + 1, c).start()
        else:
            genewise(c)

    for c in range(CHUNKS):
        product(c)
        if c == 0:
            pl.semaphore_wait(barrier, devices - 1)
        exchange(0, c).start()
        if c:
            after(0, c - 1)
    after(0, CHUNKS - 1)
    for wave in range(CHUNKS + levels - 2):
        for t in range(1, levels):
            c = wave - (t - 1)
            if 0 <= c < CHUNKS:
                after(t, c)

    total = functools.reduce(lambda a, b: a + b, totals)
    lane = lax.broadcasted_iota(jnp.int32, total.shape, 1)
    total = jnp.where(lane < half, total, total * total)
    for j in range(n_samp):
        block[j] = total[j * gene_dev:(j + 1) * gene_dev]

    slot = my_boot * n_samp + place

    def spread(o):
        there = target(o)
        pltpu.make_async_remote_copy(
            src_ref=block.at[there[1]],
            dst_ref=gathered.at[slot],
            send_sem=spread_send,
            recv_sem=spread_recv,
            device_id=there,
            device_id_type=MESH,
        ).start()

    others(spread)
    gathered[pl.ds(slot, 1)] = block[pl.ds(me, 1)]
    whole = gathered.at[pl.ds(0, devices - 1)]
    pltpu.make_async_copy(whole, whole, spread_recv).wait()

    count = float(devices * rows)
    mine = pl.ds(my_boot * n_samp, n_samp)
    for g in range(gene_dev):
        both = gathered[:, g, :]
        skat, square = both[:, :half], both[:, half:]
        own = gathered[mine, g, :]
        real = lax.broadcasted_iota(jnp.int32, skat.shape, 1) < rows
        skat_mean = jnp.sum(skat, keepdims=True) / count
        square_mean = jnp.sum(square, keepdims=True) / count
        skat_off = jnp.where(real, skat - skat_mean, 0.0)
        square_off = jnp.where(real, square - square_mean, 0.0)
        own_skat = own[:, :half] - skat_mean
        own_square = own[:, half:] - square_mean
        best = None
        for k in range(RHOS):
            rho = k / (RHOS - 1)
            off = (1.0 - rho) * skat_off + rho * square_off
            spread_k = jnp.sum(off * off, keepdims=True) / count
            score = ((1.0 - rho) * own_skat + rho * own_square) / jnp.sqrt(spread_k + EPSILON)
            best = score if best is None else jnp.maximum(best, score)
        out_ref[g] = best

    for t in range(levels):
        for c in range(CHUNKS):
            exchange(t, c).wait_send()
    pltpu.make_async_copy(whole, whole, spread_send).wait()


def shards(dosage, residuals, maf_bin, gene_map, gene_order):
    n_boot, n_samp = lax.axis_size("boot"), lax.axis_size("samp")
    samples, variants = dosage.shape
    boot_local = residuals.shape[1]
    genes = gene_order.shape[0]
    gene_dev = genes // n_samp
    rows = boot_local // n_samp
    rows_p = up(rows, 8)
    half = 64 if rows <= 64 else up(rows, 128)
    levels = n_samp.bit_length() - 1
    width = variants // CHUNKS
    vmem = pl.BlockSpec(memory_space=pltpu.VMEM)
    hbm = pl.BlockSpec(memory_space=pl.ANY)
    best = pl.pallas_call(
        functools.partial(kernel, n_boot, n_samp, rows, half),
        name="skato",
        out_shape=jax.ShapeDtypeStruct((gene_dev, n_samp, half), jnp.float32),
        in_specs=[hbm, hbm, vmem, vmem, vmem],
        out_specs=vmem,
        scratch_shapes=[
            pltpu.VMEM((samples, variants), jnp.bfloat16),
            pltpu.VMEM((samples, boot_local), jnp.bfloat16),
            pltpu.VMEM((CHUNKS, n_samp, rows_p, width), jnp.float32),
            *[
                pltpu.VMEM((CHUNKS, n_samp >> (t + 1), rows_p, width), jnp.float32)
                for t in range(levels)
            ],
            pltpu.VMEM((2 * half, width), jnp.float32),
            pltpu.VMEM((n_samp, gene_dev, 2 * half), jnp.float32),
            pltpu.VMEM((n_boot * n_samp, gene_dev, 2 * half), jnp.float32),
            pltpu.SemaphoreType.DMA((1 + CHUNKS,)),
            pltpu.SemaphoreType.DMA((levels, CHUNKS)),
            pltpu.SemaphoreType.DMA((levels, CHUNKS)),
            pltpu.SemaphoreType.DMA,
            pltpu.SemaphoreType.DMA,
        ],
        compiler_params=pltpu.CompilerParams(
            collective_id=0, has_side_effects=True, vmem_limit_bytes=60 * 1024 * 1024
        ),
    )(dosage, residuals, maf_bin[None, :], gene_map[None, :], gene_order[None, :])
    return best[:, :, :rows].reshape(gene_dev, boot_local)


def solution(mesh):
    placed = (P("samp", None), P("samp", "boot"), P(), P(), P())
    return jax.shard_map(
        shards, mesh=mesh, in_specs=placed, out_specs=P("samp", "boot"), check_vma=False
    )
```

time: 129 us -> 35.4 us (0.27)
  waiting for transfers between devices: 96.9 us -> 0 us
  Pallas kernels: 0 us -> 33.7 us
  between operations: 13.4 us -> 0.01 us
  blocking collectives: 8.14 us -> 0 us
  matrix products: 5.49 us -> 0 us
  other arithmetic: 3.86 us -> 0 us
    psum x1 -> x0, waiting for transfers between devices: 96.9 us -> none  [shards(): scores = lax.psum(partial_value, 'samp')]
    pallas_call x0 -> x1, Pallas kernels: none -> 33.7 us  [shards(): pl.pallas_call(functools.partial(kernel, n_boot, n_samp, rows, half), nam...]
    psum x1 -> x0, blocking collectives: 8.14 us -> none  [shards(): lax.psum((jnp.sum(mixtures, axis=2), jnp.sum(mixtures * mixtures, axis=2)...]
    dot_general x2 -> x0, matrix products: 5.49 us -> none  [the longest x1 4.52 us: sample_product(): lax.dot_general(dose_part, residuals, (((0,), (0,)), ((), ())), preferred...]
    mul x2 -> x0, other arithmetic: 1.96 us -> none  [the longest x1 1.95 us: shards(): stacked = jnp.concatenate([scores, scores * scores], axis=1)]
    reshape x0 -> x1, local copies, waits for them, and re-layouts: none -> 1.4 us  [shards(): return best[:, :, :rows].reshape(gene_dev, boot_local)]
  transfers between devices with their start and end apart: 1 -> 0, of which waited for: 1 -> 0; matrix products, arithmetic and copies ran while one was open for 0% -> 0% of each run, Pallas kernels for 0% -> 0%
where the time goes in v1:
time: 35.4 us; the launch traced here: 35.2 us
  Pallas kernels  33.7 us (95%)
  local copies, waits for them, and re-layouts  1.4 us (4%)
    pallas_call x1, Pallas kernels, shards(): pl.pallas_call(functools.partial(kernel, n_boot, n_samp, rows, half), nam...  33.7 us
    reshape x1, local copies, waits for them, and re-layouts, shards(): return best[:, :, :rows].reshape(gene_dev, boot_local)  1.4 us

profile of v1, /device:TPU:0, one launch (start us, length us, event | category | flops | bytes accessed | tf_op | source)
XLA Modules:
  0.0 35.2 jit_solution(14690003442935380854)
XLA Ops:
  0.0 33.7 %skato.1 = f32[2,16,64]{2,1,0:T(8,128)} custom-call(bf16[2024,512]{1,0:T(8,128)(2,1)} %dose_hbm.1, bf16[2024,640]{1,0:T(8,128)(2,1)} %resid_hbm.1, s32[1,512]{1,0:T(1,128)} %bitcast.5, s32[1,512]{1,0:T(1,128)} %bitcast.6, s32[1,32]{1,0:T(1,128)} %bitcast.7), custom_call_target="tpu_custom_call" | custom-call | tf_op jit(solution)/shard_map/skato/pallas_call | solution.py:238
  33.7 1.4 %reshape.3 = f32[2,640]{1,0:T(2,128)} reshape(f32[2,16,40]{2,1,0:T(8,128)} %bitcast.4) | data formatting | bytes 10240 | tf_op jit(solution)/shard_map/reshape | solution.py:265

commit v2 on v1

v2 whole, which is shorter than its diff:
```python
import functools
import math

import jax
import jax.numpy as jnp
from jax import lax
from jax.experimental import pallas as pl
from jax.experimental.pallas import tpu as pltpu
from jax.sharding import PartitionSpec as P

RHOS = 11
MAF_BINS = 64
EPSILON = 1e-05
MESH = pl.DeviceIdType.MESH


def up(value, unit):
    return (value + unit - 1) // unit * unit


def chunking(rows):
    for count in range(rows // 8, 0, -1):
        if rows % (8 * count) == 0:
            return count
    return 1


def bit_order(kind, levels):
    if kind == 0 or levels < 3:
        return tuple(range(levels))
    return (0, *range(2, levels), 1)


def place_of(samp, order):
    size = 1 << len(order)
    return sum((samp // (1 << bit) % 2) * (size >> (t + 1)) for t, bit in enumerate(order))


def schedule(kinds, levels):
    steps, turn = [], 0
    for c, kind in enumerate(kinds):
        if kind == 0:
            begin = 2.6 + 1.4 * turn
            turn += 1
            times = [begin + 2.6 * (t - 1) for t in range(1, levels)]
        else:
            times = [4.0 + 2.7 * (t - 1) for t in range(1, levels)]
        steps += [(time, t, c) for t, time in enumerate(times, 1)]
    return [(t, c) for _, t, c in sorted(steps)]


def kernel(
    n_boot,
    n_samp,
    rows,
    half,
    kinds,
    dose_hbm,
    resid_hbm,
    maf_ref,
    map_ref,
    order_ref,
    out_ref,
    dose,
    resid,
    acc,
    *rest,
):
    levels = n_samp.bit_length() - 1
    chunks = len(kinds)
    orders = [bit_order(kind, levels) for kind in kinds]
    landed = rest[:levels]
    stacked, block, gathered = rest[levels:levels + 3]
    load_sem, send_sem, recv_sem, spread_send, spread_recv = rest[levels + 3:]
    devices = n_boot * n_samp
    variants = dose.shape[1]
    width = resid.shape[1] // chunks
    genes = order_ref.shape[1]
    gene_dev = genes // n_samp
    rows_p = acc.shape[2]
    my_boot = lax.axis_index("boot")
    me = lax.axis_index("samp")
    linear = my_boot * n_samp + me
    bits = [lax.rem(me // (1 << t), 2) for t in range(levels)]
    partners = [me + (1 - 2 * bits[t]) * (1 << t) for t in range(levels)]

    loads = [pltpu.make_async_copy(dose_hbm, dose, load_sem.at[0])]
    for c in range(chunks):
        cols = pl.ds(c * width, width)
        loads.append(
            pltpu.make_async_copy(resid_hbm.at[:, cols], resid.at[:, cols], load_sem.at[1 + c])
        )
    for load in loads:
        load.start()

    barrier = pltpu.get_barrier_semaphore()
    for t in range(levels):
        pl.semaphore_signal(
            barrier, inc=1, device_id=(my_boot, partners[t]), device_id_type=MESH
        )
    for o in range(1, n_boot):
        pl.semaphore_signal(
            barrier, inc=1, device_id=(lax.rem(my_boot + o, n_boot), me), device_id_type=MESH
        )

    person_total = resid.shape[0] * n_samp
    base = 1.0 - 0.05 * (maf_ref[...].astype(jnp.float32) + 0.5) / MAF_BINS
    p2 = base * base
    p4 = p2 * p2
    p8 = p4 * p4
    weight = p8 * p8 * p8 / math.sqrt(person_total)
    order_row = order_ref[...].astype(jnp.float32)
    diagonal = lax.broadcasted_iota(jnp.int32, (genes, genes), 0) == lax.broadcasted_iota(
        jnp.int32, (genes, genes), 1
    )
    order_col = jnp.sum(
        jnp.where(diagonal, jnp.broadcast_to(order_row, (genes, genes)), 0.0), axis=1, keepdims=True
    )
    member = jnp.where(order_col == map_ref[...].astype(jnp.float32), 1.0, 0.0)

    lows, places = [], []
    for order in orders:
        low, line = 0, []
        for t, bit in enumerate(order):
            line.append(low)
            low = low + bits[bit] * (n_samp >> (t + 1))
        lows.append(line)
        places.append(low)
    natural = place_of(me, bit_order(0, levels))

    def exchange(t, c):
        size = n_samp >> (t + 1)
        bit = orders[c][t]
        return pltpu.make_async_remote_copy(
            src_ref=acc.at[c, pl.ds(lows[c][t] + (1 - bits[bit]) * size, size)],
            dst_ref=landed[t].at[c],
            send_sem=send_sem.at[t, c],
            recv_sem=recv_sem.at[t, c],
            device_id=(my_boot, partners[bit]),
            device_id_type=MESH,
        )

    def product(c):
        loads[1 + c].wait()
        part = lax.dot_general(
            resid[:, c * width:(c + 1) * width],
            dose[...],
            (((0,), (0,)), ((), ())),
            preferred_element_type=jnp.float32,
        )
        if rows_p != rows:
            acc[c] = jnp.zeros((n_samp, rows_p, variants), jnp.float32)
        for s in range(n_samp):
            n = place_of(s, bit_order(0, levels))
            acc[c, place_of(s, orders[c]), :rows] = part[n * rows:(n + 1) * rows]

    def fold(t, c):
        exchange(t, c).wait_recv()
        size = n_samp >> (t + 1)
        keep = pl.ds(lows[c][t] + bits[orders[c][t]] * size, size)
        acc[c, keep] = acc[c, keep] + landed[t][c]

    finished, totals = [], []

    def genewise(late):
        totals.append(
            lax.dot_general(
                member,
                stacked[late],
                (((1,), (1,)), ((), ())),
                precision=lax.Precision.HIGHEST,
                preferred_element_type=jnp.float32,
            )
        )

    def after(t, c):
        fold(t, c)
        if t + 1 < levels:
            exchange(t + 1, c).start()
            return
        scores = acc[c, pl.ds(places[c], 1)].reshape(rows_p, variants) * weight
        late = int(len(finished) == chunks - 1)
        finished.append(c)
        stacked[late, c * rows_p:(c + 1) * rows_p] = scores * scores
        stacked[late, half + c * rows_p:half + (c + 1) * rows_p] = scores
        if late or len(finished) == chunks - 1:
            genewise(late)

    stacked[...] = jnp.zeros(stacked.shape, jnp.float32)
    loads[0].wait()
    for c in range(chunks):
        product(c)
        if c == 0:
            pl.semaphore_wait(barrier, levels + n_boot - 1)
        exchange(0, c).start()
        if c:
            after(0, c - 1)
    after(0, chunks - 1)
    for t, c in schedule(kinds, levels):
        after(t, c)

    total = functools.reduce(lambda a, b: a + b, totals)
    lane = lax.broadcasted_iota(jnp.int32, total.shape, 1)
    total = jnp.where(lane < half, total, total * total)
    for j in range(n_samp):
        block[j] = total[j * gene_dev:(j + 1) * gene_dev]

    slot = my_boot * n_samp + natural

    def spread(o):
        other = lax.rem(linear + o, devices)
        there = (other // n_samp, lax.rem(other, n_samp))
        pltpu.make_async_remote_copy(
            src_ref=block.at[there[1]],
            dst_ref=gathered.at[slot],
            send_sem=spread_send,
            recv_sem=spread_recv,
            device_id=there,
            device_id_type=MESH,
        ).start()

    if devices <= 32:
        for o in range(1, devices):
            spread(o)
    else:
        lax.fori_loop(1, devices, lambda o, carry: (spread(o), carry)[1], 0)
    gathered[pl.ds(slot, 1)] = block[pl.ds(me, 1)]
    for t in range(levels):
        for c in range(chunks):
            exchange(t, c).wait_send()
    local = resid.shape[1]
    shape = (half, local)
    resample = lax.broadcasted_iota(jnp.int32, shape, 1)
    held = lax.div(resample, width) * rows_p + lax.rem(resample, rows)
    picked = jnp.where(held == lax.broadcasted_iota(jnp.int32, shape, 0), 1.0, 0.0)
    shape = (n_samp, local)
    resample = lax.broadcasted_iota(jnp.int32, shape, 1)
    owner = lax.div(lax.rem(resample, width), rows)
    owned = owner == lax.broadcasted_iota(jnp.int32, shape, 0)
    whole = gathered.at[pl.ds(0, devices - 1)]
    pltpu.make_async_copy(whole, whole, spread_recv).wait()

    count = float(devices * chunks * rows)
    mine = pl.ds(my_boot * n_samp, n_samp)
    for g in range(gene_dev):
        both = gathered[:, g, :]
        skat, square = both[:, :half], both[:, half:]
        own = gathered[mine, g, :]
        lane = lax.broadcasted_iota(jnp.int32, skat.shape, 1)
        real = (lax.rem(lane, rows_p) < rows) & (lane < chunks * rows_p)
        skat_mean = jnp.sum(skat, keepdims=True) / count
        square_mean = jnp.sum(square, keepdims=True) / count
        skat_off = jnp.where(real, skat - skat_mean, 0.0)
        square_off = jnp.where(real, square - square_mean, 0.0)
        own_skat = own[:, :half] - skat_mean
        own_square = own[:, half:] - square_mean
        best = None
        for k in range(RHOS):
            rho = k / (RHOS - 1)
            off = (1.0 - rho) * skat_off + rho * square_off
            spread_k = jnp.sum(off * off, keepdims=True) / count
            score = ((1.0 - rho) * own_skat + rho * own_square) / jnp.sqrt(spread_k + EPSILON)
            best = score if best is None else jnp.maximum(best, score)
        placed = lax.dot_general(
            best,
            picked,
            (((1,), (0,)), ((), ())),
            precision=lax.Precision.HIGHEST,
            preferred_element_type=jnp.float32,
        )
        out_ref[g:g + 1] = jnp.sum(jnp.where(owned, placed, 0.0), axis=0, keepdims=True)

    pltpu.make_async_copy(whole, whole, spread_send).wait()


def shards(dosage, residuals, maf_bin, gene_map, gene_order):
    n_boot, n_samp = lax.axis_size("boot"), lax.axis_size("samp")
    samples, variants = dosage.shape
    boot_local = residuals.shape[1]
    genes = gene_order.shape[0]
    gene_dev = genes // n_samp
    chunks = chunking(boot_local // n_samp)
    rows = boot_local // n_samp // chunks
    rows_p = up(rows, 8)
    half = 64 if chunks * rows_p <= 64 else up(chunks * rows_p, 128)
    levels = n_samp.bit_length() - 1
    kinds = tuple(int(c in (1, 3)) for c in range(chunks))
    vmem = pl.BlockSpec(memory_space=pltpu.VMEM)
    hbm = pl.BlockSpec(memory_space=pl.ANY)
    return pl.pallas_call(
        functools.partial(kernel, n_boot, n_samp, rows, half, kinds),
        name="skato",
        out_shape=jax.ShapeDtypeStruct((gene_dev, boot_local), jnp.float32),
        in_specs=[hbm, hbm, vmem, vmem, vmem],
        out_specs=vmem,
        scratch_shapes=[
            pltpu.VMEM((samples, variants), jnp.bfloat16),
            pltpu.VMEM((samples, boot_local), jnp.bfloat16),
            pltpu.VMEM((chunks, n_samp, rows_p, variants), jnp.float32),
            *[
                pltpu.VMEM((chunks, n_samp >> (t + 1), rows_p, variants), jnp.float32)
                for t in range(levels)
            ],
            pltpu.VMEM((2, 2 * half, variants), jnp.float32),
            pltpu.VMEM((n_samp, gene_dev, 2 * half), jnp.float32),
            pltpu.VMEM((n_boot * n_samp, gene_dev, 2 * half), jnp.float32),
            pltpu.SemaphoreType.DMA((1 + chunks,)),
            pltpu.SemaphoreType.DMA((levels, chunks)),
            pltpu.SemaphoreType.DMA((levels, chunks)),
            pltpu.SemaphoreType.DMA,
            pltpu.SemaphoreType.DMA,
        ],
        compiler_params=pltpu.CompilerParams(
            collective_id=0, has_side_effects=True, vmem_limit_bytes=60 * 1024 * 1024
        ),
    )(dosage, residuals, maf_bin[None, :], gene_map[None, :], gene_order[None, :])


def solution(mesh):
    placed = (P("samp", None), P("samp", "boot"), P(), P(), P())
    return jax.shard_map(
        shards, mesh=mesh, in_specs=placed, out_specs=P("samp", "boot"), check_vma=False
    )
```

time: 35.4 us -> 30.3 us (0.86)
  Pallas kernels: 33.7 us -> 28.8 us
    pallas_call x1, Pallas kernels: 33.7 us -> 28.8 us  [shards(): pl.pallas_call(functools.partial(kernel, n_boot, n_samp, rows, half, kind...]
    reshape x1 -> x0, local copies, waits for them, and re-layouts: 1.4 us -> none  [shards(): return best[:, :, :rows].reshape(gene_dev, boot_local)]
    unnamed x0 -> x1, local copies, waits for them, and re-layouts: none -> 1.28 us
where the time goes in v2:
time: 30.3 us; the launch traced here: 30.1 us
  Pallas kernels  28.8 us (95%)
  local copies, waits for them, and re-layouts  1.28 us (4%)
    pallas_call x1, Pallas kernels, shards(): pl.pallas_call(functools.partial(kernel, n_boot, n_samp, rows, half, kind...  28.8 us
    unnamed x1, local copies, waits for them, and re-layouts  1.28 us

profile of v2, /device:TPU:0, one launch (start us, length us, event | category | flops | bytes accessed | tf_op | source)
XLA Modules:
  0.0 30.1 jit_solution(10278404930830141596)
XLA Ops:
  0.0 28.8 %skato.1 = f32[2,640]{1,0:T(2,128)} custom-call(bf16[2024,512]{1,0:T(8,128)(2,1)} %dose_hbm.1, bf16[2024,640]{1,0:T(8,128)(2,1)} %resid_hbm.1, s32[1,512]{1,0:T(1,128)} %bitcast.3, s32[1,512]{1,0:T(1,128)} %bitcast.4, s32[1,32]{1,0:T(1,128)} %bitcast.5), custom_call_target="tpu_custom_call" | custom-call | tf_op jit(solution)/shard_map/skato/pallas_call | solution.py:290
  28.8 1.3 %copy.7 = f32[2,640]{1,0:T(2,128)} copy(f32[2,640]{1,0:T(2,128)} %skato.1) | data formatting | bytes 10240

commit v3 on v2

--- a/solution.py
+++ b/solution.py
@@ -25,27 +25,19 @@
     return 1
 
 
-def bit_order(kind, levels):
-    if kind == 0 or levels < 3:
-        return tuple(range(levels))
-    return (0, *range(2, levels), 1)
-
-
-def place_of(samp, order):
-    size = 1 << len(order)
-    return sum((samp // (1 << bit) % 2) * (size >> (t + 1)) for t, bit in enumerate(order))
-
-
-def schedule(kinds, levels):
-    steps, turn = [], 0
-    for c, kind in enumerate(kinds):
-        if kind == 0:
-            begin = 2.6 + 1.4 * turn
-            turn += 1
-            times = [begin + 2.6 * (t - 1) for t in range(1, levels)]
-        else:
-            times = [4.0 + 2.7 * (t - 1) for t in range(1, levels)]
-        steps += [(time, t, c) for t, time in enumerate(times, 1)]
+def phases_of(levels):
+    groups = [(bit,) for bit in range(min(2, levels))]
+    bit = 2
+    while bit < levels:
+        groups.append(tuple(range(bit, min(bit + 2, levels))))
+        bit += 2
+    return groups
+
+
+def schedule(chunks, phases):
+    steps = [
+        (2.6 + 1.4 * c + 3.5 * (t - 1), t, c) for c in range(chunks) for t in range(1, phases)
+    ]
     return [(t, c) for _, t, c in sorted(steps)]
 
 
@@ -54,7 +46,7 @@
     n_samp,
     rows,
     half,
-    kinds,
+    chunks,
     dose_hbm,
     resid_hbm,
     maf_ref,
@@ -67,11 +59,11 @@
     *rest,
 ):
     levels = n_samp.bit_length() - 1
-    chunks = len(kinds)
-    orders = [bit_order(kind, levels) for kind in kinds]
-    landed = rest[:levels]
-    stacked, block, gathered = rest[levels:levels + 3]
-    load_sem, send_sem, recv_sem, spread_send, spread_recv = rest[levels + 3:]
+    groups = phases_of(levels)
+    phases = len(groups)
+    landed = rest[:phases]
+    stacked, block, gathered = rest[phases:phases + 3]
+    load_sem, send_sem, recv_sem, spread_send, spread_recv = rest[phases + 3:]
     devices = n_boot * n_samp
     variants = dose.shape[1]
     width = resid.shape[1] // chunks
@@ -82,7 +74,25 @@
     me = lax.axis_index("samp")
     linear = my_boot * n_samp + me
     bits = [lax.rem(me // (1 << t), 2) for t in range(levels)]
-    partners = [me + (1 - 2 * bits[t]) * (1 << t) for t in range(levels)]
+    flips = [(1 - 2 * bits[t]) * (1 << t) for t in range(levels)]
+    moves = [list(range((1 << len(group)) - 1, 0, -1)) for group in groups]
+
+    def partner(t, move):
+        return me + sum(flips[bit] for i, bit in enumerate(groups[t]) if move >> i & 1)
+
+    def digit(t, move):
+        return sum(
+            ((1 - bits[bit]) if move >> i & 1 else bits[bit]) * (1 << (len(groups[t]) - 1 - i))
+            for i, bit in enumerate(groups[t])
+        )
+
+    sizes, lows, low, size = [], [], 0, n_samp
+    for t, group in enumerate(groups):
+        size >>= len(group)
+        sizes.append(size)
+        lows.append(low)
+        low = low + digit(t, 0) * size
+    natural = low
 
     loads = [pltpu.make_async_copy(dose_hbm, dose, load_sem.at[0])]
     for c in range(chunks):
@@ -94,10 +104,11 @@
         load.start()
 
     barrier = pltpu.get_barrier_semaphore()
-    for t in range(levels):
-        pl.semaphore_signal(
-            barrier, inc=1, device_id=(my_boot, partners[t]), device_id_type=MESH
-        )
+    for t in range(phases):
+        for move in moves[t]:
+            pl.semaphore_signal(
+                barrier, inc=1, device_id=(my_boot, partner(t, move)), device_id_type=MESH
+            )
     for o in range(1, n_boot):
         pl.semaphore_signal(
             barrier, inc=1, device_id=(lax.rem(my_boot + o, n_boot), me), device_id_type=MESH
@@ -118,27 +129,19 @@
     )
     member = jnp.where(order_col == map_ref[...].astype(jnp.float32), 1.0, 0.0)
 
-    lows, places = [], []
-    for order in orders:
-        low, line = 0, []
-        for t, bit in enumerate(order):
-            line.append(low)
-            low = low + bits[bit] * (n_samp >> (t + 1))
-        lows.append(line)
-        places.append(low)
-    natural = place_of(me, bit_order(0, levels))
-
-    def exchange(t, c):
-        size = n_samp >> (t + 1)
-        bit = orders[c][t]
+    def exchange(t, c, move):
         return pltpu.make_async_remote_copy(
-            src_ref=acc.at[c, pl.ds(lows[c][t] + (1 - bits[bit]) * size, size)],
-            dst_ref=landed[t].at[c],
-            send_sem=send_sem.at[t, c],
-            recv_sem=recv_sem.at[t, c],
-            device_id=(my_boot, partners[bit]),
+            src_ref=acc.at[c, pl.ds(lows[t] + digit(t, move) * sizes[t], sizes[t])],
+            dst_ref=landed[t].at[c, move - 1],
+            send_sem=send_sem.at[t, c, move - 1],
+            recv_sem=recv_sem.at[t, c, move - 1],
+            device_id=(my_boot, partner(t, move)),
             device_id_type=MESH,
         )
+
+    def send(t, c):
+        for move in moves[t]:
+            exchange(t, c, move).start()
 
     def product(c):
         loads[1 + c].wait()
@@ -150,15 +153,18 @@
         )
         if rows_p != rows:
             acc[c] = jnp.zeros((n_samp, rows_p, variants), jnp.float32)
-        for s in range(n_samp):
-            n = place_of(s, bit_order(0, levels))
-            acc[c, place_of(s, orders[c]), :rows] = part[n * rows:(n + 1) * rows]
+            for n in range(n_samp):
+                acc[c, n, :rows] = part[n * rows:(n + 1) * rows]
+        else:
+            acc[c] = part.reshape(n_samp, rows, variants)
 
     def fold(t, c):
-        exchange(t, c).wait_recv()
-        size = n_samp >> (t + 1)
-        keep = pl.ds(lows[c][t] + bits[orders[c][t]] * size, size)
-        acc[c, keep] = acc[c, keep] + landed[t][c]
+        keep = pl.ds(lows[t] + digit(t, 0) * sizes[t], sizes[t])
+        running = acc[c, keep]
+        for move in reversed(moves[t]):
+            exchange(t, c, move).wait_recv()
+            running = running + landed[t][c, move - 1]
+        acc[c, keep] = running
 
     finished, totals = [], []
 
@@ -175,10 +181,10 @@
 
     def after(t, c):
         fold(t, c)
-        if t + 1 < levels:
-            exchange(t + 1, c).start()
+        if t + 1 < phases:
+            send(t + 1, c)
             return
-        scores = acc[c, pl.ds(places[c], 1)].reshape(rows_p, variants) * weight
+        scores = acc[c, pl.ds(natural, 1)].reshape(rows_p, variants) * weight
         late = int(len(finished) == chunks - 1)
         finished.append(c)
         stacked[late, c * rows_p:(c + 1) * rows_p] = scores * scores
@@ -191,12 +197,12 @@
     for c in range(chunks):
         product(c)
         if c == 0:
-            pl.semaphore_wait(barrier, levels + n_boot - 1)
-        exchange(0, c).start()
+            pl.semaphore_wait(barrier, sum(len(m) for m in moves) + n_boot - 1)
+        send(0, c)
         if c:
             after(0, c - 1)
     after(0, chunks - 1)
-    for t, c in schedule(kinds, levels):
+    for t, c in schedule(chunks, phases):
         after(t, c)
 
     total = functools.reduce(lambda a, b: a + b, totals)
@@ -207,27 +213,38 @@
 
     slot = my_boot * n_samp + natural
 
-    def spread(o):
-        other = lax.rem(linear + o, devices)
-        there = (other // n_samp, lax.rem(other, n_samp))
+    def spread_to(boot, samp):
         pltpu.make_async_remote_copy(
-            src_ref=block.at[there[1]],
+            src_ref=block.at[samp],
             dst_ref=gathered.at[slot],
             send_sem=spread_send,
             recv_sem=spread_recv,
-            device_id=there,
+            device_id=(boot, samp),
             device_id_type=MESH,
         ).start()
 
+    def spread(o):
+        other = lax.rem(linear + o, devices)
+        spread_to(other // n_samp, lax.rem(other, n_samp))
+
     if devices <= 32:
-        for o in range(1, devices):
-            spread(o)
+        boots = [lax.rem(my_boot + o, n_boot) for o in range(n_boot)]
+        flipped, there = (1 << levels) - 1, me + sum(flips)
+        for i in range(n_samp):
+            for o in range(n_boot - 1, -1, -1):
+                if o or flipped:
+                    spread_to(boots[o], there)
+            if i + 1 < n_samp:
+                bit = ((i + 1) & -(i + 1)).bit_length() - 1
+                there = there - flips[bit] if flipped >> bit & 1 else there + flips[bit]
+                flipped ^= 1 << bit
     else:
         lax.fori_loop(1, devices, lambda o, carry: (spread(o), carry)[1], 0)
     gathered[pl.ds(slot, 1)] = block[pl.ds(me, 1)]
-    for t in range(levels):
+    for t in range(phases):
         for c in range(chunks):
-            exchange(t, c).wait_send()
+            for move in moves[t]:
+                exchange(t, c, move).wait_send()
     local = resid.shape[1]
     shape = (half, local)
     resample = lax.broadcasted_iota(jnp.int32, shape, 1)
@@ -284,11 +301,13 @@
     rows_p = up(rows, 8)
     half = 64 if chunks * rows_p <= 64 else up(chunks * rows_p, 128)
     levels = n_samp.bit_length() - 1
-    kinds = tuple(int(c in (1, 3)) for c in range(chunks))
+    groups = phases_of(levels)
+    fan = max(len(group) for group in groups)
+    taken = [sum(len(group) for group in groups[:t + 1]) for t in range(len(groups))]
     vmem = pl.BlockSpec(memory_space=pltpu.VMEM)
     hbm = pl.BlockSpec(memory_space=pl.ANY)
     return pl.pallas_call(
-        functools.partial(kernel, n_boot, n_samp, rows, half, kinds),
+        functools.partial(kernel, n_boot, n_samp, rows, half, chunks),
         name="skato",
         out_shape=jax.ShapeDtypeStruct((gene_dev, boot_local), jnp.float32),
         in_specs=[hbm, hbm, vmem, vmem, vmem],
@@ -298,15 +317,17 @@
             pltpu.VMEM((samples, boot_local), jnp.bfloat16),
             pltpu.VMEM((chunks, n_samp, rows_p, variants), jnp.float32),
             *[
-                pltpu.VMEM((chunks, n_samp >> (t + 1), rows_p, variants), jnp.float32)
-                for t in range(levels)
+                pltpu.VMEM(
+                    (chunks, (1 << len(group)) - 1, n_samp >> bits, rows_p, variants), jnp.float32
+                )
+                for group, bits in zip(groups, taken)
             ],
             pltpu.VMEM((2, 2 * half, variants), jnp.float32),
             pltpu.VMEM((n_samp, gene_dev, 2 * half), jnp.float32),
             pltpu.VMEM((n_boot * n_samp, gene_dev, 2 * half), jnp.float32),
             pltpu.SemaphoreType.DMA((1 + chunks,)),
-            pltpu.SemaphoreType.DMA((levels, chunks)),
-            pltpu.SemaphoreType.DMA((levels, chunks)),
+            pltpu.SemaphoreType.DMA((len(groups), chunks, (1 << fan) - 1)),
+            pltpu.SemaphoreType.DMA((len(groups), chunks, (1 << fan) - 1)),
             pltpu.SemaphoreType.DMA,
             pltpu.SemaphoreType.DMA,
         ],

time: 30.3 us -> 29.6 us (0.977)
  Pallas kernels: 28.8 us -> 28.1 us
    pallas_call x1, Pallas kernels: 28.8 us -> 28.1 us  [shards(): pl.pallas_call(functools.partial(kernel, n_boot, n_samp, rows, half, chun...]
where the time goes in v3:
time: 29.6 us; the launch traced here: 29.4 us
  Pallas kernels  28.1 us (95%)
  local copies, waits for them, and re-layouts  1.28 us (4%)
    pallas_call x1, Pallas kernels, shards(): pl.pallas_call(functools.partial(kernel, n_boot, n_samp, rows, half, chun...  28.1 us
    unnamed x1, local copies, waits for them, and re-layouts  1.28 us

profile of v3, /device:TPU:0, one launch (start us, length us, event | category | flops | bytes accessed | tf_op | source)
XLA Modules:
  0.0 29.4 jit_solution(7927435853465558241)
XLA Ops:
  0.0 28.1 %skato.1 = f32[2,640]{1,0:T(2,128)} custom-call(bf16[2024,512]{1,0:T(8,128)(2,1)} %dose_hbm.1, bf16[2024,640]{1,0:T(8,128)(2,1)} %resid_hbm.1, s32[1,512]{1,0:T(1,128)} %bitcast.3, s32[1,512]{1,0:T(1,128)} %bitcast.4, s32[1,32]{1,0:T(1,128)} %bitcast.5), custom_call_target="tpu_custom_call" | custom-call | tf_op jit(solution)/shard_map/skato/pallas_call | solution.py:309
  28.1 1.3 %copy.7 = f32[2,640]{1,0:T(2,128)} copy(f32[2,640]{1,0:T(2,128)} %skato.1) | data formatting | bytes 10240
